TPU v7x, 512 devices: a whole 4x4x16 slice. The times are simulated.
512 devices in a mesh: lat: 16 (over z_hi, y, core), lon: 32 (over x, z_lo).
Axes of the slice: x: 4, y: 4, z: 16 (z_hi: 2, z_lo: 8; z = z_hi * 8 + z_lo), core: 2. Of those that a mesh axis runs over, the one named last changes fastest.
Arguments:
- bands: bfloat16 [16, 256, 320, 512], P('lat', 'lon'), may hold values from -6 to 6
- avail: int32 [16, 256, 10], P('lat', 'lon'), may hold values from 0 to 1, as said below
- latent_query: bfloat16 [4, 512], replicated, may hold values from -3 to 3
- w_band: bfloat16 [512, 1024], replicated, may hold values from -3.0935922 to 3.0935922
- w_mix: bfloat16 [512, 1536], replicated, may hold values from -3 to 3
- w_out: bfloat16 [512, 512], replicated, may hold values from -0.19921875 to 0.19921875
- offsets: int32 [5, 2], replicated, may hold values from -1 to 1, as said below
Outputs:
- encoded: bfloat16 [16, 256, 4, 512], P('lat', 'lon')
Inputs may be any that keep to these rules, and one draw needn't show every extreme that they name: `avail`: each patch has at least one available block. `offsets`: row 0 is (0, 0), rows 1 and 2 are (0, -1) and (0, 1), row 3 has latitude offset -1 and row 4 latitude offset +1; all rows differ.
All inputs are finite; a program needn't handle non-finite values.
Results may differ from a plain program's by a relative error of at most 0.03.
The roundings to bfloat16 on the way count: a program that leaves them out, or rounds other values in their place, can miss the bound.
Values may be sent and summed in bfloat16 or wider, within the bound.
No kernel may reach another device: no remote copies, remote signals or barrier semaphores. Data moves between devices by JAX's collectives and lax.ppermute only.
A program may use at most 64 MiB of HBM per device.

v0:
```python
import jax
import jax.numpy as jnp
from jax import lax
from jax.sharding import PartitionSpec as P

D = 512
HEADS = 16
HEAD = 32
BANDS = 320
BLOCK = 32
LATENTS = 4
NOFF = 5


EPS = 1e-06
NEG = -1e30


def padded(cells, sides, width):
    for axis, dim in sides:
        count = lax.axis_size(axis)
        head = lax.slice_in_dim(cells, 0, width, axis=dim)
        tail = lax.slice_in_dim(cells, cells.shape[dim] - width, cells.shape[dim], axis=dim)
        cells = jnp.concatenate(
            [
                lax.ppermute(tail, axis, [(i, (i + 1) % count) for i in range(count)]),
                cells,
                lax.ppermute(head, axis, [((i + 1) % count, i) for i in range(count)]),
            ],
            axis=dim,
        )
    return cells


def rms_rows(values):
    values = values.astype(jnp.float32)
    return values * lax.rsqrt(jnp.mean(values * values, axis=-1, keepdims=True) + EPS)


def softmax_weights(scores):
    peak_value = jnp.max(scores, axis=-1, keepdims=True)
    exponent = jnp.exp(scores - peak_value)
    return (exponent / jnp.sum(exponent, axis=-1, keepdims=True)).astype(jnp.bfloat16)


def per_device(bands, avail, latent_query, w_band, w_mix, w_out, offsets):
    columns = bands.shape[1]
    groups = HEADS // 2
    half_width = D // 2
    score_scale = HEAD ** (-0.5)
    normed = rms_rows(bands[0]).astype(jnp.bfloat16)
    key_value = jnp.dot(normed.reshape(-1, D), w_band, preferred_element_type=jnp.float32).astype(
        jnp.bfloat16
    )
    key_value = key_value.reshape(columns, BANDS, 2, HEADS, HEAD)
    queries = latent_query.reshape(LATENTS, HEADS, HEAD)
    scores = (
        jnp.einsum(
            "lhe,pbhe->plhb", queries, key_value[:, :, 0], preferred_element_type=jnp.float32
        )
        * score_scale
    )
    open_band = jnp.repeat(avail[0], BLOCK, axis=-1) > 0
    scores = jnp.where(open_band[:, None, None, :], scores, NEG)
    weights = softmax_weights(scores)
    pooled = jnp.einsum(
        "plhb,pbhe->plhe", weights, key_value[:, :, 1], preferred_element_type=jnp.float32
    )
    latent = pooled.reshape(columns, LATENTS, D) + latent_query.astype(jnp.float32)
    normal = rms_rows(latent)[None]
    mixture = jnp.dot(
        normal.astype(jnp.bfloat16).reshape(-1, D), w_mix, preferred_element_type=jnp.float32
    ).astype(jnp.bfloat16)
    mixture = mixture.reshape(1, columns, LATENTS, 3 * D)
    lat_queries = mixture[..., :D].reshape(1, columns, LATENTS, HEADS, HEAD)
    near_pairs = mixture[..., D : 2 * D]
    zonal_pairs = mixture[..., 2 * D :]
    framed = padded(near_pairs, (("lat", 0), ("lon", 1)), 1)
    zonal_row = lax.all_gather(zonal_pairs, "lon", axis=1, tiled=True)
    lat_index = lax.axis_index("lat")
    lat_count = lax.axis_size("lat")
    zero_index = jnp.zeros((), jnp.int32)
    near_keys = []
    near_open = []
    for offset_slot in range(NOFF):
        step_lat = offsets[offset_slot, 0]
        step_lon = offsets[offset_slot, 1]
        shifted = lax.dynamic_slice(
            framed, (1 + step_lat, 1 + step_lon, zero_index, zero_index), (1, columns, LATENTS, D)
        )
        near_keys.append(shifted)
        target = lat_index + step_lat
        near_open.append((target >= 0) & (target < lat_count))
    near_keys = jnp.stack(near_keys, axis=2).reshape(1, columns, NOFF * LATENTS, 2, groups, HEAD)
    open_keys = jnp.repeat(jnp.stack(near_open), LATENTS)
    scores = (
        jnp.einsum(
            "ijqhe,ijkhe->ijhqk",
            lat_queries[..., :groups, :],
            near_keys[..., 0, :, :],
            preferred_element_type=jnp.float32,
        )
        * score_scale
    )
    scores = jnp.where(open_keys, scores, NEG)
    weights = softmax_weights(scores)
    near_out = jnp.einsum(
        "ijhqk,ijkhe->ijqhe", weights, near_keys[..., 1, :, :], preferred_element_type=jnp.float32
    )
    row_keys = zonal_row.reshape(1, -1, 2, groups, HEAD)
    scores = (
        jnp.einsum(
            "ijqhe,ikhe->ijhqk",
            lat_queries[..., groups:, :],
            row_keys[:, :, 0],
            preferred_element_type=jnp.float32,
        )
        * score_scale
    )
    weights = softmax_weights(scores)
    zonal_out = jnp.einsum(
        "ijhqk,ikhe->ijqhe", weights, row_keys[:, :, 1], preferred_element_type=jnp.float32
    )
    attended = jnp.concatenate(
        [
            near_out.reshape(1, columns, LATENTS, half_width),
            zonal_out.reshape(1, columns, LATENTS, half_width),
        ],
        axis=-1,
    ).astype(jnp.bfloat16)
    update = jnp.dot(attended.reshape(-1, D), w_out, preferred_element_type=jnp.float32).reshape(
        1, columns, LATENTS, D
    )
    return (normal + update).astype(jnp.bfloat16)


def solution(mesh):
    return jax.shard_map(
        per_device,
        mesh=mesh,
        in_specs=(P("lat", "lon", None, None), P("lat", "lon", None), P(), P(), P(), P(), P()),
        out_specs=P("lat", "lon", None, None),
        check_vma=False,
    )
```

profile of v0, /device:TPU:24, one launch (start us, length us, event | category | flops | bytes accessed | tf_op | source)
XLA Modules:
  0.0 315.4 jit_solution(1022444642513698989)
XLA Ops:
  6.5 0.9 reshape.192
  7.4 0.8 add.179
  8.2 2.3 multiply_reduce_fusion
  10.6 2.4 fusion.2
  13.0 4.7 %convolution_convert_fusion = bf16[2560,1024]{1,0:T(8,128)(2,1)} fusion(bf16[2560,512]{1,0:T(8,128)(2,1)S(1)} %fusion.2, bf16[512,1024]{1,0:T(8,128)(2,1)S(1)} %copy-done.5), kind=kOutput, calls=%fused_computation.2 | convolution fusion | flops 2686976000 | bytes 8912896 | tf_op jit(solution)/shard_map/dot_general | solution.py:52
  17.7 7.7 %copy.58 = bf16[2560,1024]{0,1:T(8,128)(2,1)} copy(bf16[2560,1024]{1,0:T(8,128)(2,1)} %convolution_convert_fusion) | data formatting | bytes 10485760 | tf_op jit(solution)/shard_map/convert_element_type | solution.py:52
  25.4 10.9 %reshape.191 = bf16[8,320,2,16,32]{1,0,4,3,2:T(8,128)(2,1)} reshape(bf16[2560,1024]{0,1:T(8,128)(2,1)} %copy.58) | data formatting | bytes 10485760 | tf_op jit(solution)/shard_map/reshape | solution.py:55
  36.2 6.5 %fusion.32 = (bf16[8,320,1,16,32]{1,0,4,3,2:T(8,128)(2,1)}, bf16[8,320,1,16,32]{1,0,4,3,2:T(8,128)(2,1)}) fusion(bf16[8,320,2,16,32]{1,0,4,3,2:T(8,128)(2,1)} %reshape.191), kind=kLoop, calls=%fused_computation.65 | loop fusion | bytes 10485760 | tf_op jit(solution)/shard_map/slice | solution.py:59
  43.0 2.8 fusion.39
  45.8 3.3 %multiply_reduce_fusion.1 = (f32[8,4]{1,0:T(8,128)S(1)}, f32[8,4,16,32]{3,1,2,0:T(4,128)S(1)}) fusion(f32[4,16,32]{2,0,1:T(4,128)S(1)} %copy.64, bf16[8,320,1,16,32]{1,0,4,3,2:T(8,128)(2,1)} %get-tuple-element.6, f32[8,4,16,320]{3,1,0,2:T(4,128)S(1)} %get-tuple-element.28, f32[8,4,16]{1,0,2:T(8,128)S(1)} %get-tuple-element.27), kind=kOutput, calls=%fused_computation.41 | convolution fusion | flops 10862560 | bytes 3352704 | tf_op jit(solution)/shard_map/plhb,pbhe->plhe/dot_general | solution.py:66
  49.9 1.9 collective-permute-start
  51.8 3.6 %collective-permute-start.1 = (bf16[1,8,4,512]{3,1,2,0:T(8,128)(2,1)S(1)}, bf16[1,8,4,512]{3,1,2,0:T(8,128)(2,1)S(1)}, u32[]{:S(2)}, u32[]{:S(2)}) collective-permute-start(bf16[1,8,4,512]{3,1,2,0:T(8,128)(2,1)S(1)} %copy.87), channel_id=1, source_target_pairs={{32,0},{64,32},{96,64},{128,96},{160,128},{192,160},{224,192},{256... | collective-permute-start | bytes 98312 | tf_op jit(solution)/shard_map/ppermute | solution.py:28
  55.5 0.6 slice.101
  56.4 11.6 %collective-permute-done.1 = bf16[1,8,4,512]{3,1,2,0:T(8,128)(2,1)S(1)} collective-permute-done((bf16[1,8,4,512]{3,1,2,0:T(8,128)(2,1)S(1)}, bf16[1,8,4,512]{3,1,2,0:T(8,128)(2,1)S(1)}, u32[]{:S(2)}, u32[]{:S(2)}) %collective-permute-start.1) | collective-permute-done | bytes 32800 | tf_op jit(solution)/shard_map/ppermute | solution.py:28
  68.0 2.9 collective-permute-start.2
  71.0 11.8 %collective-permute-start.3 = (bf16[3,1,4,512]{3,1,2,0:T(2,128)(2,1)S(1)}, bf16[3,1,4,512]{3,1,2,0:T(2,128)(2,1)S(1)}, u32[]{:S(2)}, u32[]{:S(2)}) collective-permute-start(bf16[3,1,4,512]{3,1,2,0:T(2,128)(2,1)S(1)} %get-tuple-element.14), channel_id=1, source_target_pairs={{1,0},{2,1},{3,2},{4,3},{5,4},{6,5},{7,6},{8,7},{9,8},{10,9},{11,1... | collective-permute-start | bytes 36872 | tf_op jit(solution)/shard_map/ppermute | solution.py:28
  82.8 0.7 fusion.38
  100.5 0.5 fusion.41
  101.5 189.4 %all-gather.2.cloned.1.call-done = bf16[1,256,4,512]{3,2,0,1:T(4,128)(2,1)} async-done(((bf16[1,8,4,512]{3,2,0,1:T(4,128)(2,1)}), bf16[1,256,4,512]{3,2,0,1:T(4,128)(2,1)}) %all-gather.2.cloned.1.call-update) | async-done | bytes 1048592 | tf_op jit(solution)/shard_map/all_gather | solution.py:79
  290.9 6.0 %reshape.202 = bf16[1,1024,2,8,32]{4,3,2,1,0:T(8,128)(2,1)} reshape(bf16[1,256,4,512]{3,2,0,1:T(4,128)(2,1)} %all-gather.2.cloned.1.call-done) | data formatting | bytes 2097152 | tf_op jit(solution)/shard_map/reshape | solution.py:110
  296.9 4.5 %fusion.33 = (bf16[1,1024,1,8,32]{4,3,2,1,0:T(8,128)(2,1)}, bf16[1,1024,1,8,32]{4,3,2,1,0:T(8,128)(2,1)}) fusion(bf16[1,1024,2,8,32]{4,3,2,1,0:T(8,128)(2,1)} %reshape.202), kind=kLoop, calls=%fused_computation.66 | loop fusion | bytes 2097152 | tf_op jit(solution)/shard_map/slice | solution.py:115
  301.4 2.5 copy.93
  303.8 2.5 copy.92
  307.9 0.6 copy.79
  (64 shorter events, 4.6 us)
Async XLA Ops:
  6.5 42.8 %copy-start = (bf16[512,1536]{1,0:T(8,128)(2,1)S(1)}, bf16[512,1536]{1,0:T(8,128)(2,1)}, u32[]{:S(2)}) copy-start(bf16[512,1536]{1,0:T(8,128)(2,1)} %param.11) | copy-start | bytes 4718596
  6.5 284.4 %all-gather.2.cloned.1.call-start = ((), (), s32[]{:S(2)}) async-start(), calls=%async_computation | async-start | bytes 1081344 | tf_op jit(solution)/shard_map/all_gather | solution.py:79
  10.5 2.5 copy-start.5
  36.2 6.5 %copy-start.4 = (s32[1,8,10]{2,1,0:T(8,128)S(1)}, s32[1,8,10]{2,1,0:T(8,128)}, u32[]{:S(2)}) copy-start(s32[1,8,10]{2,1,0:T(8,128)} %param.8) | copy-start | bytes 964
  45.8 3.5 %copy-start.2 = (bf16[4,512]{1,0:T(4,128)(2,1)S(1)}, bf16[4,512]{1,0:T(4,128)(2,1)}, u32[]{:S(2)}) copy-start(bf16[4,512]{1,0:T(4,128)(2,1)} %param.9) | copy-start | bytes 12292
  49.1 33.7 %copy-start.3 = (s32[5,2]{0,1:T(2,128)S(1)}, s32[5,2]{0,1:T(2,128)}, u32[]{:S(2)}) copy-start(s32[5,2]{0,1:T(2,128)} %param.13) | copy-start | bytes 124
  49.9 6.4 %collective-permute-start = (bf16[1,8,4,512]{3,1,2,0:T(8,128)(2,1)S(1)}, bf16[1,8,4,512]{3,1,2,0:T(8,128)(2,1)S(1)}, u32[]{:S(2)}, u32[]{:S(2)}) collective-permute-start(bf16[1,8,4,512]{3,1,2,0:T(8,128)(2,1)S(1)} %copy.87), channel_id=1, source_target_pairs={{0,32},{32,64},{64,96},{96,128},{128,160},{160,192},{192,224},{224... | collective-permute-start | bytes 98312 | tf_op jit(solution)/shard_map/ppermute | solution.py:26
  51.8 16.2 %collective-permute-start.1 = (bf16[1,8,4,512]{3,1,2,0:T(8,128)(2,1)S(1)}, bf16[1,8,4,512]{3,1,2,0:T(8,128)(2,1)S(1)}, u32[]{:S(2)}, u32[]{:S(2)}) collective-permute-start(bf16[1,8,4,512]{3,1,2,0:T(8,128)(2,1)S(1)} %copy.87), channel_id=1, source_target_pairs={{32,0},{64,32},{96,64},{128,96},{160,128},{192,160},{224,192},{256... | collective-permute-start | bytes 98312 | tf_op jit(solution)/shard_map/ppermute | solution.py:28
  68.0 31.7 %collective-permute-start.2 = (bf16[3,1,4,512]{3,1,2,0:T(2,128)(2,1)S(1)}, bf16[3,1,4,512]{3,1,2,0:T(2,128)(2,1)S(1)}, u32[]{:S(2)}, u32[]{:S(2)}) collective-permute-start(bf16[3,1,4,512]{3,1,2,0:T(2,128)(2,1)S(1)} %get-tuple-element.13), channel_id=1, source_target_pairs={{0,1},{1,2},{2,3},{3,4},{4,5},{5,6},{6,7},{7,8},{8,9},{9,10},{10,1... | collective-permute-start | bytes 36872 | tf_op jit(solution)/shard_map/ppermute | solution.py:26
  71.0 28.7 %collective-permute-start.3 = (bf16[3,1,4,512]{3,1,2,0:T(2,128)(2,1)S(1)}, bf16[3,1,4,512]{3,1,2,0:T(2,128)(2,1)S(1)}, u32[]{:S(2)}, u32[]{:S(2)}) collective-permute-start(bf16[3,1,4,512]{3,1,2,0:T(2,128)(2,1)S(1)} %get-tuple-element.14), channel_id=1, source_target_pairs={{1,0},{2,1},{3,2},{4,3},{5,4},{6,5},{7,6},{8,7},{9,8},{10,9},{11,1... | collective-permute-start | bytes 36872 | tf_op jit(solution)/shard_map/ppermute | solution.py:28
  306.7 1.0 copy-start.1
Sparse Core Ops, SparseCore 0:
  56.2 234.6 all-gather.1
where the time goes:
time: 317 us; the launch traced here: 315 us
  waiting for transfers between devices  201 us (63%)
  local copies, waits for them, and re-layouts  46.6 us (15%)
  between operations  29.4 us (9%)
  starting transfers between devices  20.3 us (6%)
  matrix products  13 us (4%)
  other arithmetic  5.12 us (2%)
    all_gather x1, waiting for transfers between devices, per_device(): zonal_row = lax.all_gather(zonal_pairs, 'lon', axis=1, tiled=True)  189 us
    ppermute x2, starting transfers between devices, padded(): lax.ppermute(head, axis, [((i + 1) % count, i) for i in range(count)])  15.4 us
    ppermute x2, waiting for transfers between devices, padded(): lax.ppermute(head, axis, [((i + 1) % count, i) for i in range(count)])  11.6 us
    reshape x1, local copies, waits for them, and re-layouts, per_device(): key_value = key_value.reshape(columns, BANDS, 2, HEADS, HEAD)  10.9 us
    convert_element_type x1, local copies, waits for them, and re-layouts, per_device(): jnp.dot(normed.reshape(-1, D), w_band, preferred_element_type=jnp.float32)  7.68 us
    slice x1, local copies, waits for them, and re-layouts, per_device(): key_value[:, :, 0]  6.54 us
  transfers between devices with their start and end apart: 5, of which 2 were waited for; matrix products, arithmetic and copies ran while one was open for 1% of the time, Pallas kernels for 0%

commit v1 on v0

v1 whole, which is shorter than its diff:
```python
import jax
import jax.numpy as jnp
from jax import lax
from jax.experimental import pallas as pl
from jax.experimental.pallas import tpu as pltpu
from jax.sharding import Mesh, PartitionSpec as P

D = 512
HEADS = 16
HEAD = 32
BANDS = 320
BLOCK = 32
LATENTS = 4
NBLK = 10
HALF = D // 2
GROUPS = HEADS // 2
COLS = 8
TOK = COLS * LATENTS
LON = 32
LAT = 16
SCALE = HEAD ** (-0.5)

EPS = 1e-06
NEG = -1e30

LON_AXES = ("x", "q", "m", "p")
CLASS_AXES = ("x", "m")

F32 = jnp.float32
BF16 = jnp.bfloat16
CONTRACT_LAST = (((1,), (1,)), ((), ()))


def iota(shape, dim):
    return lax.broadcasted_iota(jnp.int32, shape, dim)


def rms(values):
    return values * lax.rsqrt(jnp.mean(values * values, axis=-1, keepdims=True) + EPS)


def softmax_weights(scores):
    exponent = jnp.exp(scores - jnp.max(scores, axis=-1, keepdims=True))
    return (exponent / jnp.sum(exponent, axis=-1, keepdims=True)).astype(BF16)


def lon_index():
    return lax.axis_index("x") * 8 + lax.axis_index("q") * 4 + lax.axis_index("m") * 2 + lax.axis_index("p")


PER_STEP = 2


def pool_kernel(
    avail_ref, bands_ref, query_ref, w_band_ref, w_mix_hbm, send_ref, normal_ref, near_ref, nearq_ref,
    qbd_ref, latent_ref, w_mix_ref, halo_ref, sem,
):
    step = pl.program_id(0)
    w_mix_copy = pltpu.make_async_copy(w_mix_hbm, w_mix_ref, sem)
    query = query_ref[...].astype(F32)

    @pl.when(step == 0)
    def _():
        w_mix_copy.start()
        own_head = iota((HEADS, D), 1) // HEAD == iota((HEADS, D), 0)
        for l in range(LATENTS):
            row = jnp.broadcast_to(query[l : l + 1], (HEADS, D))
            qbd_ref[l * HEADS : (l + 1) * HEADS, :] = jnp.where(own_head, row, 0.0).astype(BF16)

    own_lane = iota((HEADS, D), 1) // HEAD == iota((HEADS, D), 0)
    band_block = iota((1, BANDS), 1) // BLOCK
    tokens = bands_ref[0].reshape(PER_STEP * BANDS, D).astype(F32)
    normed = rms(tokens).astype(BF16)
    key_value = jnp.dot(normed, w_band_ref[...], preferred_element_type=F32).astype(BF16)
    for i in range(PER_STEP):
        patch = step * PER_STEP + i
        rows = slice(i * BANDS, (i + 1) * BANDS)
        scores = (
            lax.dot_general(qbd_ref[...], key_value[rows, :D], CONTRACT_LAST, preferred_element_type=F32)
            * SCALE
        )
        is_open = jnp.zeros((1, BANDS), jnp.int32)
        for b in range(NBLK):
            is_open = jnp.where(band_block == b, avail_ref[0, patch, b], is_open)
        scores = jnp.where(is_open > 0, scores, NEG)
        weights = softmax_weights(scores)
        pooled = jnp.dot(weights, key_value[rows, D:], preferred_element_type=F32)
        for l in range(LATENTS):
            part = jnp.where(own_lane, pooled[l * HEADS : (l + 1) * HEADS], 0.0)
            latent_ref[step, i * LATENTS + l : i * LATENTS + l + 1, :] = (
                jnp.sum(part, axis=0, keepdims=True) + query[l : l + 1]
            )

    @pl.when(step == COLS // PER_STEP - 1)
    def _():
        w_mix_copy.wait()
        normal = rms(latent_ref[...].reshape(TOK, D))
        normal_ref[...] = normal
        mixture = jnp.dot(normal.astype(BF16), w_mix_ref[...], preferred_element_type=F32)
        near_ref[...] = mixture[:, D : 2 * D].astype(BF16)
        nearq_ref[...] = mixture[:, :HALF].astype(BF16)
        for side, first in ((0, 0), (1, TOK - LATENTS)):
            for j in range(4):
                halo_ref[side, j * LATENTS : (j + 1) * LATENTS, :] = mixture[
                    first : first + LATENTS, D + j * 128 : D + (j + 1) * 128
                ]
        to_west = halo_ref[0].astype(BF16)
        to_east = halo_ref[1].astype(BF16)
        me = lon_index()
        east = lax.rem(me + 1, LON)
        west = lax.rem(me + LON - 1, LON)
        half = TOK // 2
        zeros = jnp.zeros((half, HEAD), F32)
        for g in range(GROUPS):
            q = mixture[:, HALF + g * HEAD : HALF + (g + 1) * HEAD]
            k = mixture[:, 2 * D + g * HEAD : 2 * D + (g + 1) * HEAD]
            v = mixture[:, 2 * D + HALF + g * HEAD : 2 * D + HALF + (g + 1) * HEAD]
            pairs = jnp.concatenate([k[:half], v[:half], k[half:], v[half:]], axis=1).astype(BF16)
            slot = jnp.concatenate([q[:half], zeros, q[half:], zeros], axis=1).astype(BF16)
            for c in range(4):
                dest = (g // 2) * 8 + (c // 2) * 4 + (g % 2) * 2 + c % 2
                send_ref[dest, :half, :] = pairs
                send_ref[dest, half:, :] = jnp.where(dest == east, to_east, jnp.where(dest == west, to_west, slot))


def pool(bands, avail, latent_query, w_band, w_mix):
    whole = lambda *shape: pl.BlockSpec(shape, lambda i: (0,) * len(shape))
    return pl.pallas_call(
        pool_kernel,
        grid=(COLS // PER_STEP,),
        in_specs=[
            pl.BlockSpec(memory_space=pltpu.SMEM),
            pl.BlockSpec((1, PER_STEP, BANDS, D), lambda i: (0, i, 0, 0)),
            whole(LATENTS, D),
            whole(D, 2 * D),
            pl.BlockSpec(memory_space=pl.ANY),
        ],
        out_specs=[whole(LON, TOK, 128), whole(TOK, D), whole(TOK, D), whole(TOK, HALF)],
        out_shape=[
            jax.ShapeDtypeStruct((LON, TOK, 128), BF16),
            jax.ShapeDtypeStruct((TOK, D), F32),
            jax.ShapeDtypeStruct((TOK, D), BF16),
            jax.ShapeDtypeStruct((TOK, HALF), BF16),
        ],
        scratch_shapes=[
            pltpu.VMEM((LATENTS * HEADS, D), BF16),
            pltpu.VMEM((COLS // PER_STEP, PER_STEP * LATENTS, D), F32),
            pltpu.VMEM((D, 3 * D), BF16),
            pltpu.VMEM((2, 16, 128), F32),
            pltpu.SemaphoreType.DMA,
        ],
        name="pool",
    )(avail, bands, latent_query, w_band, w_mix)


def window_kernel(offsets_ref, near_ref, got_ref, own_ref, up_ref, down_ref, ext_ref):
    me = lon_index()
    half = TOK // 2
    west = got_ref[lax.rem(me + LON - 1, LON), half:, :].astype(F32)
    east = got_ref[lax.rem(me + 1, LON), half:, :].astype(F32)
    for j in range(4):
        lanes = slice(j * 128, (j + 1) * 128)
        ext_ref[:LATENTS, lanes] = west[j * LATENTS : (j + 1) * LATENTS]
        ext_ref[LATENTS + TOK :, lanes] = east[j * LATENTS : (j + 1) * LATENTS]
    ext_ref[LATENTS : LATENTS + TOK, :] = near_ref[...].astype(F32)
    shifted = [ext_ref[i * LATENTS : i * LATENTS + TOK, :].astype(BF16) for i in range(3)]
    own_ref[:TOK] = shifted[1]
    own_ref[TOK : 2 * TOK] = shifted[0]
    own_ref[2 * TOK :] = shifted[2]
    for ref, slot in ((down_ref, 3), (up_ref, 4)):
        step = offsets_ref[slot, 1]
        ref[...] = jnp.where(step == 0, shifted[1], jnp.where(step < 0, shifted[0], shifted[2]))


def windows(offsets, near, got):
    return pl.pallas_call(
        window_kernel,
        in_specs=[
            pl.BlockSpec(memory_space=pltpu.SMEM),
            pl.BlockSpec(memory_space=pltpu.VMEM),
            pl.BlockSpec(memory_space=pltpu.VMEM),
        ],
        out_shape=[
            jax.ShapeDtypeStruct((3 * TOK, D), BF16),
            jax.ShapeDtypeStruct((TOK, D), BF16),
            jax.ShapeDtypeStruct((TOK, D), BF16),
        ],
        scratch_shapes=[pltpu.VMEM((TOK + 2 * LATENTS, D), F32)],
        name="windows",
    )(offsets, near, got)


def zonal_kernel(got_ref, out_ref):
    half = TOK // 2
    qp = lax.axis_index("q") * 4 + lax.axis_index("p")
    pairs = got_ref[:, :half, :].reshape(LON * half, 128)
    slots = jnp.concatenate([got_ref[(c // 2) * 8 + (c % 2) * 2 + qp, half:, :] for c in range(8)], axis=0)
    slots = slots.astype(F32)
    lane = iota((8 * half, 128), 1)
    first = jnp.where(lane < HEAD, slots, 0.0)
    second = jnp.where((lane >= 64) & (lane < 64 + HEAD), slots, 0.0)
    low = jnp.concatenate([first, pltpu.roll(second, 64, 1)], axis=0).astype(BF16)
    high = jnp.concatenate([pltpu.roll(first, 64, 1), second], axis=0).astype(BF16)
    scores_low = lax.dot_general(low, pairs, CONTRACT_LAST, preferred_element_type=F32) * SCALE
    scores_high = lax.dot_general(high, pairs, CONTRACT_LAST, preferred_element_type=F32) * SCALE
    peak = jnp.maximum(
        jnp.max(scores_low, axis=-1, keepdims=True), jnp.max(scores_high, axis=-1, keepdims=True)
    )
    exp_low = jnp.exp(scores_low - peak)
    exp_high = jnp.exp(scores_high - peak)
    total = jnp.sum(exp_low, axis=-1, keepdims=True) + jnp.sum(exp_high, axis=-1, keepdims=True)
    weights_low = (exp_low / total).astype(BF16)
    weights_high = (exp_high / total).astype(BF16)
    out_low = jnp.dot(weights_low, pairs, preferred_element_type=F32)
    out_high = jnp.dot(weights_high, pairs, preferred_element_type=F32)
    rows = 8 * half
    for_first = out_low[:rows] + pltpu.roll(out_high[:rows], 64, 1)
    for_second = pltpu.roll(out_low[rows:], 64, 1) + out_high[rows:]
    out_ref[...] = jnp.where(lane < 64, for_first, for_second).astype(BF16).reshape(8, half, 128)


def zonal(got):
    return pl.pallas_call(
        zonal_kernel,
        out_shape=jax.ShapeDtypeStruct((GROUPS, TOK // 2, 128), BF16),
        name="zonal",
    )(got)


def final_kernel(own_ref, north_ref, south_ref, nearq_ref, back_ref, normal_ref, w_out_ref, out_ref, zonal_ref):
    keys = jnp.concatenate([own_ref[...], north_ref[...], south_ref[...]], axis=0)
    count = 5 * TOK
    query = nearq_ref[...]
    head_lane = iota((TOK, HALF), 1) // HEAD
    spread = jnp.concatenate(
        [jnp.where(head_lane == h, query, jnp.zeros_like(query)) for h in range(GROUPS)], axis=0
    )
    scores = lax.dot_general(spread, keys[:, :HALF], CONTRACT_LAST, preferred_element_type=F32) * SCALE
    row = iota((GROUPS * TOK, count), 0)
    col = iota((GROUPS * TOK, count), 1)
    lat = lax.axis_index("lat")
    from_lat = jnp.where(col < 3 * TOK, lat, jnp.where(col < 4 * TOK, lat - 1, lat + 1))
    same = (row % TOK) // LATENTS == (col % TOK) // LATENTS
    scores = jnp.where(same & (from_lat >= 0) & (from_lat < LAT), scores, NEG)
    weights = softmax_weights(scores)
    spread_out = jnp.dot(weights, keys[:, HALF:], preferred_element_type=F32)
    near_out = jnp.zeros((TOK, HALF), F32)
    for h in range(GROUPS):
        near_out += jnp.where(head_lane == h, spread_out[h * TOK : (h + 1) * TOK], 0.0)

    half = TOK // 2
    lane_head = iota((half, 128), 1) // HEAD
    for part in range(2):
        for tile in range(2):
            block = jnp.zeros((half, 128), F32)
            for i in range(4):
                piece = back_ref[tile * 4 + i].astype(F32)
                shift = (i * HEAD - HEAD - part * 64) % 128
                if shift:
                    piece = pltpu.roll(piece, shift, 1)
                block = jnp.where(lane_head == i, piece, block)
            zonal_ref[part * half : (part + 1) * half, tile * 128 : (tile + 1) * 128] = block.astype(BF16)
    attended = jnp.concatenate([near_out.astype(BF16), zonal_ref[...]], axis=1)
    update = jnp.dot(attended, w_out_ref[...], preferred_element_type=F32)
    encoded = (normal_ref[...] + update).astype(BF16)
    for c in range(COLS):
        out_ref[0, c] = encoded[c * LATENTS : (c + 1) * LATENTS]


def final(own, north, south, nearq, back, normal, w_out):
    return pl.pallas_call(
        final_kernel,
        out_shape=jax.ShapeDtypeStruct((1, COLS, LATENTS, D), BF16),
        scratch_shapes=[pltpu.VMEM((TOK, HALF), BF16)],
        name="final",
    )(own, north, south, nearq, back, normal, w_out)


def per_device(bands, avail, latent_query, w_band, w_mix, w_out, offsets):
    send, normal, near, nearq = pool(bands, avail, latent_query, w_band, w_mix)
    got = lax.all_to_all(send, LON_AXES, 0, 0, tiled=True)
    own, up, down = windows(offsets, near, got)
    north = lax.ppermute(down, "lat", [(i, i + 1) for i in range(LAT - 1)])
    south = lax.ppermute(up, "lat", [(i + 1, i) for i in range(LAT - 1)])
    back = lax.all_to_all(zonal(got), CLASS_AXES, 0, 0, tiled=True)
    return final(own, north, south, nearq, back, normal, w_out)


def solution(mesh):
    grid = Mesh(mesh.devices.reshape(LAT, 4, 2, 2, 2), ("lat",) + LON_AXES)
    patches = P("lat", LON_AXES, None, None)
    return jax.shard_map(
        per_device,
        mesh=grid,
        in_specs=(patches, P("lat", LON_AXES, None), P(), P(), P(), P(), P()),
        out_specs=patches,
        check_vma=False,
    )
```

time: 317 us -> 81.5 us (0.26)
  the two profiles are of different devices: /device:TPU:24 before, /device:TPU:27 now
where the time goes in v1:
time: 81.5 us; the launch traced here: 81.2 us
  blocking collectives  32.1 us (39%)
  starting transfers between devices  16.8 us (21%)
  Pallas kernels  16.6 us (20%)
  waiting for transfers between devices  14.4 us (18%)
  local copies, waits for them, and re-layouts  1.28 us (2%)
    all_to_all x1, blocking collectives, per_device(): got = lax.all_to_all(send, LON_AXES, 0, 0, tiled=True)  32.1 us
    ppermute x1, waiting for transfers between devices, per_device(): south = lax.ppermute(up, 'lat', [(i + 1, i) for i in range(LAT - 1)])  14.4 us
    pallas_call x1, Pallas kernels, pool(): pl.pallas_call(pool_kernel, grid=(COLS // PER_STEP,), in_specs=[pl.BlockS...  10 us
    ppermute x1, starting transfers between devices, per_device(): north = lax.ppermute(down, 'lat', [(i, i + 1) for i in range(LAT - 1)])  9.44 us
    all_to_all x1, starting transfers between devices, per_device(): back = lax.all_to_all(zonal(got), CLASS_AXES, 0, 0, tiled=True)  5.41 us
    pallas_call x1, Pallas kernels, final(): pl.pallas_call(final_kernel, out_shape=jax.ShapeDtypeStruct((1, COLS, LAT...  2.53 us
    pallas_call x1, Pallas kernels, zonal(): pl.pallas_call(zonal_kernel, out_shape=jax.ShapeDtypeStruct((GROUPS, TOK...  2.38 us
    ppermute x1, starting transfers between devices, per_device(): south = lax.ppermute(up, 'lat', [(i + 1, i) for i in range(LAT - 1)])  1.92 us
  transfers between devices with their start and end apart: 3, of which 1 were waited for; matrix products, arithmetic and copies ran while one was open for 1% of the time, Pallas kernels for 2%

profile of v1, /device:TPU:27, one launch (start us, length us, event | category | flops | bytes accessed | tf_op | source)
XLA Modules:
  0.0 81.2 jit_solution(2759942137334644803)
XLA Ops:
  0.0 0.0 copy-start.3
  0.0 10.0 %pool.1 = (bf16[32,32,128]{2,1,0:T(8,128)(2,1)}, f32[32,512]{1,0:T(8,128)}, bf16[32,512]{1,0:T(8,128)(2,1)}, bf16[32,256]{1,0:T(8,128)(2,1)}) custom-call(s32[1,8,10]{2,1,0:T(8,128)} %avail_ref.1, bf16[1,8,320,512]{3,2,1,0:T(8,128)(2,1)} %bands_ref.1, bf16[4,512]{1,0:T(4,128)(2,1)} %query_ref.1, bf16[512,1024]{1,0:T(8,128)(2,1)} %w_band_ref.1, ...), custom_call_target="tpu_custom_call" | custom-call | tf_op jit(solution)/shard_map/pool/pallas_call | solution.py:128
  10.0 32.1 %all_to_all.10.got_ref = bf16[32,32,128]{2,1,0:T(8,128)(2,1)} all-to-all(bf16[32,32,128]{2,1,0:T(8,128)(2,1)} %get-tuple-element.13), channel_id=1, replica_groups=mesh['lat'=16,'x'=4,'q'=2,'m'=2,'p'=2] {'x','q','m','p'}, dimensions={0} | all-to-all | bytes 524288 | tf_op jit(solution)/shard_map/all_to_all | solution.py:281
  42.1 2.4 %zonal.1 = bf16[8,16,128]{2,1,0:T(8,128)(2,1)} custom-call(bf16[32,32,128]{2,1,0:T(8,128)(2,1)} %all_to_all.10.got_ref), custom_call_target="tpu_custom_call" | custom-call | tf_op jit(solution)/shard_map/zonal/pallas_call | solution.py:223
  44.5 5.4 %all-to-all-start.1 = ((bf16[8,16,128]{2,1,0:T(8,128)(2,1)}), bf16[8,16,128]{2,1,0:T(8,128)(2,1)S(1)}, u32[]{:S(2)}, u32[]{:S(2)}) async-start(bf16[8,16,128]{2,1,0:T(8,128)(2,1)} %zonal.1), calls=%async_computation.1 | async-start | bytes 65536 | tf_op jit(solution)/shard_map/all_to_all | solution.py:285
  49.9 0.0 copy-done.3
  49.9 0.7 copy.8.offsets_ref
  50.6 1.7 %windows.1 = (bf16[96,512]{1,0:T(8,128)(2,1)}, bf16[32,512]{1,0:T(8,128)(2,1)}, bf16[32,512]{1,0:T(8,128)(2,1)}) custom-call(s32[5,2]{1,0:T(8,128)} %copy.8.offsets_ref, bf16[32,512]{1,0:T(8,128)(2,1)} %get-tuple-element.12.near_ref, bf16[32,32,128]{2,1,0:T(8,128)(2,1)} %all_to_all.10.got_ref), custom_call_target="tpu_custom_call" | custom-call | tf_op jit(solution)/shard_map/windows/pallas_call | solution.py:176
  52.3 9.4 %collective-permute-start = (bf16[32,512]{1,0:T(8,128)(2,1)}, bf16[32,512]{1,0:T(8,128)(2,1)S(1)}, u32[]{:S(2)}, u32[]{:S(2)}) collective-permute-start(bf16[32,512]{1,0:T(8,128)(2,1)} %get-tuple-element.15), channel_id=1, source_target_pairs={{0,32},{32,64},{64,96},{96,128},{128,160},{160,192},{192,224},{224... | collective-permute-start | bytes 98312 | tf_op jit(solution)/shard_map/ppermute | solution.py:283
  61.7 1.9 %collective-permute-start.1 = (bf16[32,512]{1,0:T(8,128)(2,1)}, bf16[32,512]{1,0:T(8,128)(2,1)S(1)}, u32[]{:S(2)}, u32[]{:S(2)}) collective-permute-start(bf16[32,512]{1,0:T(8,128)(2,1)} %get-tuple-element.16), channel_id=1, source_target_pairs={{32,0},{64,32},{96,64},{128,96},{160,128},{192,160},{224,192},{256... | collective-permute-start | bytes 98312 | tf_op jit(solution)/shard_map/ppermute | solution.py:284
  63.7 0.0 collective-permute-done.north_ref
  63.7 0.0 copy-start.1
  63.7 14.4 %collective-permute-done.1.south_ref = bf16[32,512]{1,0:T(8,128)(2,1)S(1)} collective-permute-done((bf16[32,512]{1,0:T(8,128)(2,1)}, bf16[32,512]{1,0:T(8,128)(2,1)S(1)}, u32[]{:S(2)}, u32[]{:S(2)}) %collective-permute-start.1) | collective-permute-done | bytes 32800 | tf_op jit(solution)/shard_map/ppermute | solution.py:284
  78.0 0.0 copy-start.2
  78.0 0.0 all-to-all-done.1.back_ref
  78.0 0.0 copy-start
  78.0 0.0 copy-done.1
  78.0 0.6 copy-done.2
  78.6 0.0 copy-done
  78.6 2.5 %final.1 = bf16[1,8,4,512]{3,2,1,0:T(4,128)(2,1)} custom-call(bf16[96,512]{1,0:T(8,128)(2,1)} %get-tuple-element.14.own_ref, bf16[32,512]{1,0:T(8,128)(2,1)} %copy-done.1, bf16[32,512]{1,0:T(8,128)(2,1)} %copy-done.2, bf16[32,256]{1,0:T(8,128)(2,1)} %get-tuple-element.17.nearq_ref, bf16[8,16,128]{2,1,0:T(8,128)(2,1)} %copy-done, ...), custom_call_target="tpu_custom_call" | custom-call | tf_op jit(solution)/shard_map/final/pallas_call | solution.py:271
Async XLA Ops:
  0.0 49.9 %copy-start.3 = (s32[5,2]{0,1:T(2,128)S(1)}, s32[5,2]{0,1:T(2,128)}, u32[]{:S(2)}) copy-start(s32[5,2]{0,1:T(2,128)} %param.13) | copy-start | bytes 124
  44.5 33.5 %all-to-all-start.1 = ((bf16[8,16,128]{2,1,0:T(8,128)(2,1)}), bf16[8,16,128]{2,1,0:T(8,128)(2,1)S(1)}, u32[]{:S(2)}, u32[]{:S(2)}) async-start(bf16[8,16,128]{2,1,0:T(8,128)(2,1)} %zonal.1), calls=%async_computation.1 | async-start | bytes 65536 | tf_op jit(solution)/shard_map/all_to_all | solution.py:285
  52.3 11.4 %collective-permute-start = (bf16[32,512]{1,0:T(8,128)(2,1)}, bf16[32,512]{1,0:T(8,128)(2,1)S(1)}, u32[]{:S(2)}, u32[]{:S(2)}) collective-permute-start(bf16[32,512]{1,0:T(8,128)(2,1)} %get-tuple-element.15), channel_id=1, source_target_pairs={{0,32},{32,64},{64,96},{96,128},{128,160},{160,192},{192,224},{224... | collective-permute-start | bytes 98312 | tf_op jit(solution)/shard_map/ppermute | solution.py:283
  61.7 16.3 %collective-permute-start.1 = (bf16[32,512]{1,0:T(8,128)(2,1)}, bf16[32,512]{1,0:T(8,128)(2,1)S(1)}, u32[]{:S(2)}, u32[]{:S(2)}) collective-permute-start(bf16[32,512]{1,0:T(8,128)(2,1)} %get-tuple-element.16), channel_id=1, source_target_pairs={{32,0},{64,32},{96,64},{128,96},{160,128},{192,160},{224,192},{256... | collective-permute-start | bytes 98312 | tf_op jit(solution)/shard_map/ppermute | solution.py:284
  63.7 14.4 %copy-start.1 = (bf16[32,512]{1,0:T(8,128)(2,1)}, bf16[32,512]{1,0:T(8,128)(2,1)S(1)}, u32[]{:S(2)}) copy-start(bf16[32,512]{1,0:T(8,128)(2,1)S(1)} %collective-permute-done.north_ref) | copy-start | bytes 98308
  78.0 0.6 copy-start.2
  78.0 0.6 copy-start

commit v2 on v1

--- a/solution.py
+++ b/solution.py
@@ -4,6 +4,7 @@
 from jax.experimental import pallas as pl
 from jax.experimental.pallas import tpu as pltpu
 from jax.sharding import Mesh, PartitionSpec as P
+
 
 D = 512
 HEADS = 16
@@ -153,7 +154,7 @@
     )(avail, bands, latent_query, w_band, w_mix)
 
 
-def window_kernel(offsets_ref, near_ref, got_ref, own_ref, up_ref, down_ref, ext_ref):
+def window_kernel(offsets_ref, near_ref, got_ref, own_ref, chip_ref, far_ref, ext_ref):
     me = lon_index()
     half = TOK // 2
     west = got_ref[lax.rem(me + LON - 1, LON), half:, :].astype(F32)
@@ -167,8 +168,13 @@
     own_ref[:TOK] = shifted[1]
     own_ref[TOK : 2 * TOK] = shifted[0]
     own_ref[2 * TOK :] = shifted[2]
-    for ref, slot in ((down_ref, 3), (up_ref, 4)):
-        step = offsets_ref[slot, 1]
+    is_even = lax.rem(lax.axis_index("lat"), 2) == 0
+    south_step = offsets_ref[1, 3]
+    north_step = offsets_ref[1, 4]
+    for ref, step in (
+        (chip_ref, jnp.where(is_even, south_step, north_step)),
+        (far_ref, jnp.where(is_even, north_step, south_step)),
+    ):
         ref[...] = jnp.where(step == 0, shifted[1], jnp.where(step < 0, shifted[0], shifted[2]))
 
 
@@ -227,8 +233,8 @@
     )(got)
 
 
-def final_kernel(own_ref, north_ref, south_ref, nearq_ref, back_ref, normal_ref, w_out_ref, out_ref, zonal_ref):
-    keys = jnp.concatenate([own_ref[...], north_ref[...], south_ref[...]], axis=0)
+def final_kernel(own_ref, chip_ref, far_ref, nearq_ref, back_ref, normal_ref, w_out_ref, out_ref, zonal_ref):
+    keys = jnp.concatenate([own_ref[...], chip_ref[...], far_ref[...]], axis=0)
     count = 5 * TOK
     query = nearq_ref[...]
     head_lane = iota((TOK, HALF), 1) // HEAD
@@ -239,9 +245,9 @@
     row = iota((GROUPS * TOK, count), 0)
     col = iota((GROUPS * TOK, count), 1)
     lat = lax.axis_index("lat")
-    from_lat = jnp.where(col < 3 * TOK, lat, jnp.where(col < 4 * TOK, lat - 1, lat + 1))
+    inside = jnp.where((lat > 0) & (lat < LAT - 1), count, 4 * TOK)
     same = (row % TOK) // LATENTS == (col % TOK) // LATENTS
-    scores = jnp.where(same & (from_lat >= 0) & (from_lat < LAT), scores, NEG)
+    scores = jnp.where(same & (col < inside), scores, NEG)
     weights = softmax_weights(scores)
     spread_out = jnp.dot(weights, keys[:, HALF:], preferred_element_type=F32)
     near_out = jnp.zeros((TOK, HALF), F32)
@@ -267,23 +273,24 @@
         out_ref[0, c] = encoded[c * LATENTS : (c + 1) * LATENTS]
 
 
-def final(own, north, south, nearq, back, normal, w_out):
+def final(own, chip, far, nearq, back, normal, w_out):
     return pl.pallas_call(
         final_kernel,
         out_shape=jax.ShapeDtypeStruct((1, COLS, LATENTS, D), BF16),
         scratch_shapes=[pltpu.VMEM((TOK, HALF), BF16)],
         name="final",
-    )(own, north, south, nearq, back, normal, w_out)
+    )(own, chip, far, nearq, back, normal, w_out)
 
 
 def per_device(bands, avail, latent_query, w_band, w_mix, w_out, offsets):
     send, normal, near, nearq = pool(bands, avail, latent_query, w_band, w_mix)
     got = lax.all_to_all(send, LON_AXES, 0, 0, tiled=True)
-    own, up, down = windows(offsets, near, got)
-    north = lax.ppermute(down, "lat", [(i, i + 1) for i in range(LAT - 1)])
-    south = lax.ppermute(up, "lat", [(i + 1, i) for i in range(LAT - 1)])
-    back = lax.all_to_all(zonal(got), CLASS_AXES, 0, 0, tiled=True)
-    return final(own, north, south, nearq, back, normal, w_out)
+    own, to_chip, to_far = windows(offsets.T, near, got)
+    far = lax.ppermute(to_far, "lat", [(i, i + 1 if i % 2 else i - 1) for i in range(1, LAT - 1)])
+    chip = lax.ppermute(to_chip, "lat", [(i, i ^ 1) for i in range(LAT)])
+    mine = zonal(got)
+    back = lax.all_to_all(mine, CLASS_AXES, 0, 0, tiled=True)
+    return final(own, chip, far, nearq, back, normal, w_out)
 
 
 def solution(mesh):

time: 81.5 us -> 75.3 us (0.924)
  waiting for transfers between devices: 14.4 us -> 8.78 us
    ppermute x2, waiting for transfers between devices: 14.4 us -> 8.78 us  [the longest x1 8.78 us: per_device(): lax.ppermute(to_far, 'lat', [(i, i + 1 if i % 2 else i - 1) for i in rang...]
  transfers between devices with their start and end apart: 3 -> 3, of which waited for: 1 -> 1; matrix products, arithmetic and copies ran while one was open for 1% -> 0% of each run, Pallas kernels for 2% -> 2%
where the time goes in v2:
time: 75.3 us; the launch traced here: 74.9 us
  blocking collectives  32.1 us (43%)
  starting transfers between devices  16.8 us (22%)
  Pallas kernels  16.6 us (22%)
  waiting for transfers between devices  8.78 us (12%)
    all_to_all x1, blocking collectives, per_device(): got = lax.all_to_all(send, LON_AXES, 0, 0, tiled=True)  32.1 us
    pallas_call x1, Pallas kernels, pool(): pl.pallas_call(pool_kernel, grid=(COLS // PER_STEP,), in_specs=[pl.BlockS...  10 us
    ppermute x1, waiting for transfers between devices, per_device(): lax.ppermute(to_far, 'lat', [(i, i + 1 if i % 2 else i - 1) for i in rang...  8.78 us
    ppermute x1, starting transfers between devices, per_device(): lax.ppermute(to_far, 'lat', [(i, i + 1 if i % 2 else i - 1) for i in rang...  7.5 us
    all_to_all x1, starting transfers between devices, per_device(): back = lax.all_to_all(mine, CLASS_AXES, 0, 0, tiled=True)  5.41 us
    ppermute x1, starting transfers between devices, per_device(): chip = lax.ppermute(to_chip, 'lat', [(i, i ^ 1) for i in range(LAT)])  3.87 us
    pallas_call x1, Pallas kernels, final(): pl.pallas_call(final_kernel, out_shape=jax.ShapeDtypeStruct((1, COLS, LAT...  2.53 us
    pallas_call x1, Pallas kernels, zonal(): pl.pallas_call(zonal_kernel, out_shape=jax.ShapeDtypeStruct((GROUPS, TOK...  2.38 us
  transfers between devices with their start and end apart: 3, of which 1 were waited for; matrix products, arithmetic and copies ran while one was open for 0% of the time, Pallas kernels for 2%

profile of v2, /device:TPU:27, one launch (start us, length us, event | category | flops | bytes accessed | tf_op | source)
XLA Modules:
  0.0 74.9 jit_solution(18191743907313426122)
XLA Ops:
  0.0 10.0 %pool.1 = (bf16[32,32,128]{2,1,0:T(8,128)(2,1)}, f32[32,512]{1,0:T(8,128)}, bf16[32,512]{1,0:T(8,128)(2,1)}, bf16[32,256]{1,0:T(8,128)(2,1)}) custom-call(s32[1,8,10]{2,1,0:T(8,128)} %avail_ref.1, bf16[1,8,320,512]{3,2,1,0:T(8,128)(2,1)} %bands_ref.1, bf16[4,512]{1,0:T(4,128)(2,1)} %query_ref.1, bf16[512,1024]{1,0:T(8,128)(2,1)} %w_band_ref.1, ...), custom_call_target="tpu_custom_call" | custom-call | tf_op jit(solution)/shard_map/pool/pallas_call | solution.py:129
  10.0 32.1 %all_to_all.10.got_ref = bf16[32,32,128]{2,1,0:T(8,128)(2,1)} all-to-all(bf16[32,32,128]{2,1,0:T(8,128)(2,1)} %get-tuple-element.13), channel_id=1, replica_groups=mesh['lat'=16,'x'=4,'q'=2,'m'=2,'p'=2] {'x','q','m','p'}, dimensions={0} | all-to-all | bytes 524288 | tf_op jit(solution)/shard_map/all_to_all | solution.py:287
  42.1 2.4 %zonal.1 = bf16[8,16,128]{2,1,0:T(8,128)(2,1)} custom-call(bf16[32,32,128]{2,1,0:T(8,128)(2,1)} %all_to_all.10.got_ref), custom_call_target="tpu_custom_call" | custom-call | tf_op jit(solution)/shard_map/zonal/pallas_call | solution.py:229
  44.5 5.4 %all-to-all-start.1 = ((bf16[8,16,128]{2,1,0:T(8,128)(2,1)}), bf16[8,16,128]{2,1,0:T(8,128)(2,1)S(1)}, u32[]{:S(2)}, u32[]{:S(2)}) async-start(bf16[8,16,128]{2,1,0:T(8,128)(2,1)} %zonal.1), calls=%async_computation.1 | async-start | bytes 65536 | tf_op jit(solution)/shard_map/all_to_all | solution.py:292
  49.9 1.7 %windows.1 = (bf16[96,512]{1,0:T(8,128)(2,1)}, bf16[32,512]{1,0:T(8,128)(2,1)}, bf16[32,512]{1,0:T(8,128)(2,1)}) custom-call(s32[2,5]{1,0:T(2,128)} %bitcast.1, bf16[32,512]{1,0:T(8,128)(2,1)} %get-tuple-element.12.near_ref, bf16[32,32,128]{2,1,0:T(8,128)(2,1)} %all_to_all.10.got_ref), custom_call_target="tpu_custom_call" | custom-call | tf_op jit(solution)/shard_map/windows/pallas_call | solution.py:182
  51.6 3.9 %collective-permute-start = (bf16[32,512]{1,0:T(8,128)(2,1)}, bf16[32,512]{1,0:T(8,128)(2,1)S(1)}, u32[]{:S(2)}, u32[]{:S(2)}) collective-permute-start(bf16[32,512]{1,0:T(8,128)(2,1)} %get-tuple-element.15), channel_id=1, source_target_pairs={{0,32},{32,0},{64,96},{96,64},{128,160},{160,128},{192,224},{224,1... | collective-permute-start | bytes 98312 | tf_op jit(solution)/shard_map/ppermute | solution.py:290
  55.5 7.5 %collective-permute-start.1 = (bf16[32,512]{1,0:T(8,128)(2,1)}, bf16[32,512]{1,0:T(8,128)(2,1)S(1)}, u32[]{:S(2)}, u32[]{:S(2)}) collective-permute-start(bf16[32,512]{1,0:T(8,128)(2,1)} %get-tuple-element.16), channel_id=1, source_target_pairs={{32,64},{64,32},{96,128},{128,96},{160,192},{192,160},{224,256},{2... | collective-permute-start | bytes 98312 | tf_op jit(solution)/shard_map/ppermute | solution.py:289
  63.0 0.0 collective-permute-done.chip_ref
  63.0 0.0 copy-start.1
  63.0 8.8 %collective-permute-done.1.far_ref = bf16[32,512]{1,0:T(8,128)(2,1)S(1)} collective-permute-done((bf16[32,512]{1,0:T(8,128)(2,1)}, bf16[32,512]{1,0:T(8,128)(2,1)S(1)}, u32[]{:S(2)}, u32[]{:S(2)}) %collective-permute-start.1) | collective-permute-done | bytes 32800 | tf_op jit(solution)/shard_map/ppermute | solution.py:289
  71.8 0.0 copy-start.2
  71.8 0.0 all-to-all-done.1.back_ref
  71.8 0.0 copy-start
  71.8 0.0 copy-done.1
  71.8 0.6 copy-done.2
  72.4 0.0 copy-done
  72.4 2.5 %final.1 = bf16[1,8,4,512]{3,2,1,0:T(4,128)(2,1)} custom-call(bf16[96,512]{1,0:T(8,128)(2,1)} %get-tuple-element.14.own_ref, bf16[32,512]{1,0:T(8,128)(2,1)} %copy-done.1, bf16[32,512]{1,0:T(8,128)(2,1)} %copy-done.2, bf16[32,256]{1,0:T(8,128)(2,1)} %get-tuple-element.17.nearq_ref, bf16[8,16,128]{2,1,0:T(8,128)(2,1)} %copy-done, ...), custom_call_target="tpu_custom_call" | custom-call | tf_op jit(solution)/shard_map/final/pallas_call | solution.py:277
Async XLA Ops:
  44.5 27.3 %all-to-all-start.1 = ((bf16[8,16,128]{2,1,0:T(8,128)(2,1)}), bf16[8,16,128]{2,1,0:T(8,128)(2,1)S(1)}, u32[]{:S(2)}, u32[]{:S(2)}) async-start(bf16[8,16,128]{2,1,0:T(8,128)(2,1)} %zonal.1), calls=%async_computation.1 | async-start | bytes 65536 | tf_op jit(solution)/shard_map/all_to_all | solution.py:292
  51.6 11.4 %collective-permute-start = (bf16[32,512]{1,0:T(8,128)(2,1)}, bf16[32,512]{1,0:T(8,128)(2,1)S(1)}, u32[]{:S(2)}, u32[]{:S(2)}) collective-permute-start(bf16[32,512]{1,0:T(8,128)(2,1)} %get-tuple-element.15), channel_id=1, source_target_pairs={{0,32},{32,0},{64,96},{96,64},{128,160},{160,128},{192,224},{224,1... | collective-permute-start | bytes 98312 | tf_op jit(solution)/shard_map/ppermute | solution.py:290
  55.5 16.3 %collective-permute-start.1 = (bf16[32,512]{1,0:T(8,128)(2,1)}, bf16[32,512]{1,0:T(8,128)(2,1)S(1)}, u32[]{:S(2)}, u32[]{:S(2)}) collective-permute-start(bf16[32,512]{1,0:T(8,128)(2,1)} %get-tuple-element.16), channel_id=1, source_target_pairs={{32,64},{64,32},{96,128},{128,96},{160,192},{192,160},{224,256},{2... | collective-permute-start | bytes 98312 | tf_op jit(solution)/shard_map/ppermute | solution.py:289
  63.0 8.8 %copy-start.1 = (bf16[32,512]{1,0:T(8,128)(2,1)}, bf16[32,512]{1,0:T(8,128)(2,1)S(1)}, u32[]{:S(2)}) copy-start(bf16[32,512]{1,0:T(8,128)(2,1)S(1)} %collective-permute-done.chip_ref) | copy-start | bytes 98308
  71.8 0.6 copy-start.2
  71.8 0.6 copy-start
